TPU v7x, 32 devices: a whole 2x2x4 slice. The times are simulated.
32 devices in a mesh: grp: 2 (over core), dev: 16 (over z, y, x).
Axes of the slice: x: 2, y: 2, z: 4, core: 2. Of those that a mesh axis runs over, the one named last changes fastest.
Arguments:
- queries: float32 [32, 12, 128], P(('grp', 'dev')), may hold values from -2.1 to 2.1
- pages: float32 [32, 256, 128], P(('grp', 'dev')), may hold values from -2.1 to 2.1
- positive: int32 [32], replicated, may hold values from 0 to 31
Outputs:
- loss: float32 [], replicated
- question_token_slope: float32 [32, 12, 128], P(('grp', 'dev'))
- page_grad: float32 [32, 256, 128], P(('grp', 'dev'))
All inputs are finite; a program needn't handle non-finite values.
Results may differ from a plain program's by a relative error of at most 0.00019.
Values sent between devices are 32-bit elements; how exact they have to be, the bound alone decides.
A program may use at most 64 MiB of HBM per device.

v0:
```python
import jax
import jax.numpy as jnp
from jax import lax
from jax.sharding import PartitionSpec as P

cap_value = 4.0
sharpness_divisor = 0.25
logit_scale = 8.0
z_weight = 0.001
highest = lax.Precision.HIGHEST


def block_partial_terms(query_rows, page_rows, query_tokens):
    scores = jnp.dot(query_rows, page_rows.T, precision=highest, preferred_element_type=jnp.float32)
    tangent = jnp.tanh(scores / cap_value)
    bounded_similarity = cap_value * tangent
    exponential_grid = jnp.exp(bounded_similarity / sharpness_divisor)
    accumulated_totals = jnp.sum(exponential_grid, axis=1)
    gentle_peak = sharpness_divisor * jnp.log(accumulated_totals)
    slopes = (
        exponential_grid
        / accumulated_totals[:, None]
        * (1.0 - tangent * tangent)
        * (logit_scale / query_tokens)
    )
    return (gentle_peak, slopes)


def shards(queries, pages, positive):
    gathered = lax.all_gather(queries, ("grp", "dev"), axis=0, tiled=True)
    query_count, query_tokens, feature_width = gathered.shape
    page_rows = pages[0]
    page_index = lax.axis_index(("grp", "dev"))
    block_size = 16
    block_count = query_count // block_size
    query_blocks = gathered.reshape(block_count, block_size * query_tokens, feature_width)
    chosen = (positive == page_index).astype(jnp.float32)

    def block_logits(gentle_peak):
        return (
            logit_scale / query_tokens * gentle_peak.reshape(block_size, query_tokens).sum(axis=1)
        )

    def evaluate_loss_and_slopes(query_rows):
        gentle_peak, slopes = block_partial_terms(query_rows, page_rows, query_tokens)
        unscaled = jnp.dot(slopes, page_rows, precision=highest, preferred_element_type=jnp.float32)
        return (block_logits(gentle_peak), unscaled)

    logits, unscaled = lax.map(evaluate_loss_and_slopes, query_blocks)
    statistics_logits = logits.reshape(query_count)
    exponential_grid = jnp.exp(statistics_logits)
    accumulated_totals, matching_logit = lax.psum(
        (exponential_grid, chosen * statistics_logits), ("grp", "dev")
    )
    log_totals = jnp.log(accumulated_totals)
    loss = jnp.mean(log_totals - matching_logit + z_weight * log_totals * log_totals)
    coefficients = (
        (1.0 + 2.0 * z_weight * log_totals) * exponential_grid / accumulated_totals - chosen
    ) / query_count
    loss, coefficients = (loss, coefficients)
    factors = jnp.repeat(coefficients, query_tokens).reshape(
        block_count, block_size * query_tokens, 1
    )
    query_terms = unscaled * factors

    def page_only(page_total, inputs):
        query_rows, factor_rows = inputs
        unused_smooth, slopes = block_partial_terms(query_rows, page_rows, query_tokens)
        token_grads = slopes * factor_rows
        page_total = page_total + jnp.dot(
            token_grads.T, query_rows, precision=highest, preferred_element_type=jnp.float32
        )
        return (page_total, None)

    page_start = jnp.zeros(page_rows.shape, jnp.float32)
    page_total, unused_outputs = lax.scan(page_only, page_start, (query_blocks, factors))
    query_terms = query_terms.reshape(query_count, query_tokens, feature_width)
    summed = lax.psum(query_terms, ("grp", "dev"))
    own_count = queries.shape[0]
    question_token_slope = lax.dynamic_slice_in_dim(summed, page_index * own_count, own_count, 0)
    return (loss, question_token_slope, page_total[None])


def solution(mesh):
    return jax.shard_map(
        shards,
        mesh=mesh,
        in_specs=(P(("grp", "dev"), None, None), P(("grp", "dev"), None, None), P()),
        out_specs=(P(), P(("grp", "dev"), None, None), P(("grp", "dev"), None, None)),
        check_vma=False,
    )
```

profile of v0, /device:TPU:0, one launch (start us, length us, event | category | flops | bytes accessed | tf_op | source)
XLA Modules:
  0.0 258.3 jit_solution(4730078051259543547)
XLA Ops:
  7.2 0.7 copy-done.1
  7.9 71.4 %all_gather.3 = f32[32,12,128]{2,1,0:T(8,128)S(1)} all-gather(f32[1,12,128]{2,1,0:T(8,128)S(1)} %copy.13), channel_id=1, replica_groups=mesh['grp'=2,'dev'=16] {'grp','dev'}, dimensions={0}, use_global_device_ids=true | all-gather | bytes 202752 | tf_op jit(solution)/shard_map/all_gather | solution.py:30
  79.3 0.9 copy-done
  80.2 2.2 while.27
  80.2 0.4 fusion.57
  80.7 0.4 fusion.58
  81.2 0.1 reduce_sum.54
  81.3 0.4 fusion.57
  81.8 0.4 fusion.58
  82.3 0.1 reduce_sum.54
  82.5 0.7 copy-done.2
  83.2 36.8 %all-reduce = (f32[32]{0:T(128)S(1)}, f32[32]{0:T(128)S(1)}) all-reduce(f32[32]{0:T(128)S(1)} %get-tuple-element.208, f32[32]{0:T(128)S(1)} %get-tuple-element.207), channel_id=1, replica_groups=mesh['grp'=2,'dev'=16] {'grp','dev'}, use_global_device_ids=true, to_apply=%region_5.6 | all-reduce | flops 64 | bytes 512 | tf_op jit(solution)/shard_map/psum | solution.py:52
  120.0 0.6 fusion.39
  120.7 0.1 broadcast_in_dim.36
  120.8 0.1 broadcast_multiply_fusion
  121.0 0.7 reshape.47
  121.8 2.5 while.28
  121.8 0.4 fusion.62
  122.3 0.8 convolution_add_fusion.2
  123.1 0.4 fusion.62
  123.5 0.8 convolution_add_fusion.2
  125.0 124.0 %all-reduce.3.cloned.1.call-done = f32[32,12,128]{2,1,0:T(8,128)} async-done(((f32[32,12,128]{2,1,0:T(8,128)}), f32[32,12,128]{2,1,0:T(8,128)}) %all-reduce.3.cloned.1.call-update) | async-done | bytes 196624 | tf_op jit(solution)/shard_map/psum | solution.py:78
  249.0 0.7 constant_dynamic-slice_fusion
  249.7 0.6 copy.15
  (27 shorter events, 0.7 us)
Async XLA Ops:
  7.2 241.8 %all-reduce.3.cloned.1.call-start = ((), (), s32[]{:S(2)}) async-start(), calls=%async_computation | async-start | bytes 524288 | tf_op jit(solution)/shard_map/psum | solution.py:78
  7.2 0.7 copy-start.1
  79.3 0.9 copy-start
  82.5 0.7 copy-start.2
  124.3 126.0 %copy-start.3 = (f32[256,128]{1,0:T(8,128)}, f32[256,128]{1,0:T(8,128)S(1)}, u32[]{:S(2)}) copy-start(f32[256,128]{1,0:T(8,128)S(1)} %get-tuple-element.136) | copy-start | bytes 393220
Sparse Core Ops, SparseCore 0:
  121.8 127.1 all-reduce.2
where the time goes:
time: 259 us; the launch traced here: 258 us
  waiting for transfers between devices  124 us (48%)
  blocking collectives  108 us (42%)
  between operations  15.9 us (6%)
  local copies, waits for them, and re-layouts  4.91 us (2%)
  matrix products  4.08 us (2%)
    psum x1, waiting for transfers between devices, shards(): summed = lax.psum(query_terms, ('grp', 'dev'))  124 us
    all_gather x1, blocking collectives, shards(): gathered = lax.all_gather(queries, ('grp', 'dev'), axis=0, tiled=True)  71.4 us
    psum x1, blocking collectives, shards(): lax.psum((exponential_grid, chosen * statistics_logits), ('grp', 'dev'))  36.8 us
  transfers between devices with their start and end apart: 1, of which 1 were waited for; matrix products, arithmetic and copies ran while one was open for 1% of the time, Pallas kernels for 0%

commit v1 on v0

v1 whole, which is shorter than its diff:
```python
import functools
import math

import jax
import jax.numpy as jnp
from jax import lax
from jax.experimental import pallas as pl
from jax.experimental.pallas import tpu as pltpu
from jax.sharding import PartitionSpec as P

cap_value = 4.0
sharpness_divisor = 0.25
logit_scale = 8.0
z_weight = 0.001
highest = lax.Precision.HIGHEST
MESH = pl.DeviceIdType.MESH


def split(x):
    high = x.astype(jnp.bfloat16)
    low = (x - high.astype(jnp.float32)).astype(jnp.bfloat16)
    return high, low


def dot(a, b):
    return jnp.dot(a, b, preferred_element_type=jnp.float32)


def dot3(a, b):
    (a_high, a_low), (b_high, b_low) = a, b
    return dot(a_high, b_high) + (dot(a_high, b_low) + dot(a_low, b_high))


def kernel(
    groups, members, block, pad,
    query_hbm, page_hbm, positive_hbm,
    loss_ref, query_grad_hbm, page_grad_hbm,
    gathered, page, positive, rows, slopes_of, slopes_t, own_logits, logits, terms, arrived,
    weights, page_grad, query_grad,
    query_sem, page_sem, positive_sem, out_sems, send_sems, recv_sems,
):
    count = groups * members
    blocks = count // block
    tokens = gathered.shape[1]
    lanes = own_logits.shape[-1]
    block_rows = block * pad
    group, member = lax.axis_index("grp"), lax.axis_index("dev")
    me = group * members + member

    def place(k):
        peer = lax.rem(me + k, count)
        return peer, (peer // members, lax.rem(peer, members))

    query_copy = pltpu.make_async_copy(query_hbm.at[0], gathered.at[me], query_sem)
    page_copy = pltpu.make_async_copy(page_hbm.at[0], page, page_sem)
    positive_copy = pltpu.make_async_copy(positive_hbm, positive, positive_sem)
    query_copy.start()
    page_copy.start()
    positive_copy.start()

    barrier = pltpu.get_barrier_semaphore()

    def greet(k, carry):
        _, device = place(k)
        pl.semaphore_signal(barrier, inc=1, device_id=device, device_id_type=MESH)
        return carry

    lax.fori_loop(1, count, greet, 0)
    query_copy.wait()
    pl.semaphore_wait(barrier, count - 1)

    def send_query(k, carry):
        _, device = place(k)
        pltpu.make_async_remote_copy(
            gathered.at[me], gathered.at[me], send_sems.at[0], recv_sems.at[0],
            device_id=device, device_id_type=MESH,
        ).start()
        return carry

    lax.fori_loop(1, count, send_query, 0)

    def wait_all(buffer, sem):
        whole = buffer.at[pl.ds(0, count - 1)]
        pltpu.make_async_copy(whole, whole, sem).wait()

    page_copy.wait()
    positive_copy.wait()
    page_rows = page[...]
    page_columns = page_rows.T
    page_parts = split(page_rows)
    rows[...] = jnp.zeros_like(rows)
    wait_all(gathered, recv_sems.at[0])

    def score(b, logit_row):
        for q in range(block):
            rows[b, q * pad:q * pad + tokens, :] = gathered[b * block + q]
        scores = jnp.dot(
            rows[b], page_columns, precision=highest, preferred_element_type=jnp.float32
        )
        tangent = jnp.tanh(scores / cap_value)
        grid = jnp.exp(tangent * (cap_value / sharpness_divisor))
        totals = jnp.sum(grid, axis=1, keepdims=True)
        peak = sharpness_divisor * jnp.log(totals)
        slopes = grid * (1.0 - tangent * tangent) * ((logit_scale / tokens) / totals)
        slopes_of[b] = slopes
        row = lax.broadcasted_iota(jnp.int32, (block_rows, lanes), 0)
        lane = lax.broadcasted_iota(jnp.int32, (block_rows, lanes), 1)
        mine = (lane == b * block + row // pad) & (row % pad < tokens)
        return logit_row + jnp.sum(jnp.where(mine, peak, 0.0), axis=0, keepdims=True)

    logit_row = lax.fori_loop(0, blocks, score, jnp.zeros((1, lanes), jnp.float32))
    own_logits[...] = logit_row * (logit_scale / tokens)
    logits[me] = own_logits[...]

    def send_logits(k, carry):
        _, device = place(k)
        pltpu.make_async_remote_copy(
            own_logits, logits.at[me], send_sems.at[1], recv_sems.at[1],
            device_id=device, device_id_type=MESH,
        ).start()
        return carry

    lax.fori_loop(1, count, send_logits, 0)

    def project(b, carry):
        slopes = slopes_of[b]
        term = dot3(split(slopes), page_parts)
        for q in range(block):
            terms[b * block + q] = term[q * pad:q * pad + tokens, :]
        slopes_t[b] = slopes.T
        return carry

    lax.fori_loop(0, blocks, project, 0)

    def send_terms(k, carry):
        peer, device = place(k)
        pltpu.make_async_remote_copy(
            terms.at[peer], arrived.at[me], send_sems.at[2], recv_sems.at[2],
            device_id=device, device_id_type=MESH,
        ).start()
        return carry

    lax.fori_loop(1, count, send_terms, 0)

    wait_all(logits, recv_sems.at[1])
    table = logits[:, 0, :][:, :count]
    of_page = lax.broadcasted_iota(jnp.int32, (count, count), 0)
    of_query = lax.broadcasted_iota(jnp.int32, (count, count), 1)
    chosen = (positive[...] == of_page).astype(jnp.float32)
    grid = jnp.exp(table)
    totals = jnp.sum(grid, axis=0, keepdims=True)
    log_totals = jnp.log(totals)
    matching = jnp.sum(chosen * table, axis=0, keepdims=True)
    losses = log_totals - matching + z_weight * log_totals * log_totals
    loss_ref[...] = jnp.sum(losses, axis=1, keepdims=True) / count
    coefficients = ((1.0 + 2.0 * z_weight * log_totals) * grid / totals - chosen) / count
    of_me = jnp.sum(jnp.where(of_page == me, coefficients, 0.0), axis=0, keepdims=True)
    to_me = jnp.sum(jnp.where(of_query == me, coefficients, 0.0), axis=1, keepdims=True)
    weights[...] = jnp.broadcast_to(to_me, weights.shape)

    def gather_page(b, total):
        row = lax.broadcasted_iota(jnp.int32, (block_rows, count), 0)
        lane = lax.broadcasted_iota(jnp.int32, (block_rows, count), 1)
        mine = lane == b * block + row // pad
        factor = jnp.sum(jnp.where(mine, of_me, 0.0), axis=1, keepdims=True)
        return total + dot3(split(slopes_t[b]), split(rows[b] * factor))

    page_grad[...] = lax.fori_loop(0, blocks, gather_page, jnp.zeros(page_grad.shape, jnp.float32))
    page_out = pltpu.make_async_copy(page_grad, page_grad_hbm.at[0], out_sems.at[0])
    page_out.start()

    wait_all(arrived, recv_sems.at[2])
    arrived[me] = terms[me]

    def gather_query(p, total):
        return total + arrived[p] * weights[pl.ds(p, 1), :]

    query_grad[...] = lax.fori_loop(
        0, count, gather_query, jnp.zeros(query_grad.shape, jnp.float32), unroll=8
    )
    query_out = pltpu.make_async_copy(query_grad, query_grad_hbm.at[0], out_sems.at[1])
    query_out.start()
    wait_all(gathered, send_sems.at[0])
    wait_all(logits, send_sems.at[1])
    wait_all(terms, send_sems.at[2])
    page_out.wait()
    query_out.wait()


def shards(groups, members, queries, pages, positive):
    count = groups * members
    _, tokens, width = queries.shape
    page_tokens = pages.shape[1]
    block = math.gcd(count, 16)
    blocks = count // block
    pad = -(-tokens // 8) * 8
    lanes = max(128, -(-count // 128) * 128)
    anywhere = pl.BlockSpec(memory_space=pl.ANY)
    float32 = jnp.float32
    loss, query_grad, page_grad = pl.pallas_call(
        functools.partial(kernel, groups, members, block, pad),
        out_shape=(
            jax.ShapeDtypeStruct((1, 1), float32),
            jax.ShapeDtypeStruct(queries.shape, float32),
            jax.ShapeDtypeStruct(pages.shape, float32),
        ),
        in_specs=[anywhere] * 3,
        out_specs=(pl.BlockSpec(memory_space=pltpu.VMEM), anywhere, anywhere),
        scratch_shapes=[
            pltpu.VMEM((count, tokens, width), float32),
            pltpu.VMEM((page_tokens, width), float32),
            pltpu.VMEM((1, count), jnp.int32),
            pltpu.VMEM((blocks, block * pad, width), float32),
            pltpu.VMEM((blocks, block * pad, page_tokens), float32),
            pltpu.VMEM((blocks, page_tokens, block * pad), float32),
            pltpu.VMEM((1, lanes), float32),
            pltpu.VMEM((count, 1, lanes), float32),
            pltpu.VMEM((count, tokens, width), float32),
            pltpu.VMEM((count, tokens, width), float32),
            pltpu.VMEM((count, width), float32),
            pltpu.VMEM((page_tokens, width), float32),
            pltpu.VMEM((tokens, width), float32),
            pltpu.SemaphoreType.DMA,
            pltpu.SemaphoreType.DMA,
            pltpu.SemaphoreType.DMA,
            pltpu.SemaphoreType.DMA((2,)),
            pltpu.SemaphoreType.DMA((3,)),
            pltpu.SemaphoreType.DMA((3,)),
        ],
        compiler_params=pltpu.CompilerParams(collective_id=0, has_side_effects=True),
    )(queries, pages, positive.reshape(1, count))
    return loss.reshape(()), query_grad, page_grad


def solution(mesh):
    groups, members = mesh.shape["grp"], mesh.shape["dev"]
    split_spec = P(("grp", "dev"), None, None)
    return jax.shard_map(
        functools.partial(shards, groups, members),
        mesh=mesh,
        in_specs=(split_spec, split_spec, P()),
        out_specs=(P(), split_spec, split_spec),
        check_vma=False,
    )
```

time: 259 us -> 29.7 us (0.11)
  waiting for transfers between devices: 124 us -> 0 us
  blocking collectives: 108 us -> 0 us
  Pallas kernels: 0 us -> 22.8 us
  between operations: 15.9 us -> 2.4 us
  matrix products: 4.08 us -> 0 us
    psum x1 -> x0, waiting for transfers between devices: 124 us -> none  [shards(): summed = lax.psum(query_terms, ('grp', 'dev'))]
    all_gather x1 -> x0, blocking collectives: 71.4 us -> none  [shards(): gathered = lax.all_gather(queries, ('grp', 'dev'), axis=0, tiled=True)]
    psum x1 -> x0, blocking collectives: 36.8 us -> none  [shards(): lax.psum((exponential_grid, chosen * statistics_logits), ('grp', 'dev'))]
    pallas_call x0 -> x1, Pallas kernels: none -> 22.8 us  [shards(): pl.pallas_call(functools.partial(kernel, groups, members, block, pad), ou...]
    dot_general x8 -> x0, matrix products: 4.08 us -> none  [the longest x4 1.79 us: block_partial_terms(): jnp.dot(query_rows, page_rows.T, precision=highest, preferred_element_typ...]
  transfers between devices with their start and end apart: 1 -> 0, of which waited for: 1 -> 0; matrix products, arithmetic and copies ran while one was open for 1% -> 0% of each run, Pallas kernels for 0% -> 0%
where the time goes in v1:
time: 29.7 us; the launch traced here: 29.3 us
  Pallas kernels  22.8 us (77%)
  local copies, waits for them, and re-layouts  4.16 us (14%)
  between operations  2.4 us (8%)
    pallas_call x1, Pallas kernels, shards(): pl.pallas_call(functools.partial(kernel, groups, members, block, pad), ou...  22.8 us
    unnamed x3, local copies, waits for them, and re-layouts  4.16 us

profile of v1, /device:TPU:0, one launch (start us, length us, event | category | flops | bytes accessed | tf_op | source)
XLA Modules:
  0.0 29.3 jit_solution(13036382383454769986)
XLA Ops:
  0.6 1.3 %copy.6.query_hbm = f32[1,12,128]{2,1,0:T(8,128)} copy(f32[1,12,128]{2,0,1:T(1,128)} %param.3) | data formatting | bytes 12288 | tf_op args[0]
  1.9 22.8 %shard_map.58 = (f32[1,1]{1,0:T(1,128)}, f32[1,12,128]{2,1,0:T(8,128)}, f32[1,256,128]{2,1,0:T(8,128)}) custom-call(f32[1,12,128]{2,1,0:T(8,128)} %copy.6.query_hbm, f32[1,256,128]{2,1,0:T(8,128)} %page_hbm.1, s32[1,32]{1,0:T(1,128)} %bitcast.2), custom_call_target="tpu_custom_call" | custom-call | tf_op jit(solution)/shard_map/pallas_call | solution.py:200
  24.7 1.3 %copy.7 = f32[1,12,128]{2,0,1:T(1,128)} copy(f32[1,12,128]{2,1,0:T(8,128)} %get-tuple-element.10) | data formatting | bytes 12288
  26.6 1.6 %copy.11 = f32[1,256,128]{2,1,0:T(8,128)} copy(f32[1,256,128]{2,1,0:T(8,128)} %get-tuple-element.17) | data formatting | bytes 262144

commit v2 on v1

v2 whole, which is shorter than its diff:
```python
import functools
import math

import jax
import jax.numpy as jnp
from jax import lax
from jax.experimental import pallas as pl
from jax.experimental.pallas import tpu as pltpu
from jax.sharding import PartitionSpec as P

cap_value = 4.0
sharpness_divisor = 0.25
logit_scale = 8.0
z_weight = 0.001
highest = lax.Precision.HIGHEST
MESH = pl.DeviceIdType.MESH


def split(x):
    high = x.astype(jnp.bfloat16)
    low = (x - high.astype(jnp.float32)).astype(jnp.bfloat16)
    return high, low


def dot(a, b):
    return jnp.dot(a, b, preferred_element_type=jnp.float32)


def dot3(a, b):
    (a_high, a_low), (b_high, b_low) = a, b
    return dot(a_high, b_high) + (dot(a_high, b_low) + dot(a_low, b_high))


def kernel(
    groups, members, block, pad,
    query_hbm, page_hbm, positive_hbm,
    query_grad, page_grad,
    gathered, page, positive, rows, slopes_t, own_logits, logits, terms, arrived, weights,
    query_sem, page_sem, positive_sem, send_sems, recv_sems,
):
    count = groups * members
    group_blocks = members // block
    blocks = groups * group_blocks
    tokens = gathered.shape[1]
    lanes = own_logits.shape[-1]
    block_rows = block * pad
    group, member = lax.axis_index("grp"), lax.axis_index("dev")
    me = group * members + member

    query_copy = pltpu.make_async_copy(query_hbm.at[:, 0], gathered.at[me], query_sem)
    page_copy = pltpu.make_async_copy(page_hbm.at[0], page, page_sem)
    positive_copy = pltpu.make_async_copy(positive_hbm, positive, positive_sem)
    query_copy.start()
    page_copy.start()
    positive_copy.start()

    def each(first, last, act):
        def step(k, carry):
            to_group = lax.rem(group + k // members, groups)
            to_member = lax.rem(member + k, members)
            act(to_group * members + to_member, (to_group, to_member))
            return carry

        lax.fori_loop(first, last, step, 0)

    def send(source, target, stage, device):
        pltpu.make_async_remote_copy(
            source, target, send_sems.at[stage], recv_sems.at[stage],
            device_id=device, device_id_type=MESH,
        ).start()

    def wait_all(buffer, size, sem):
        whole = buffer.at[pl.ds(0, size)]
        pltpu.make_async_copy(whole, whole, sem).wait()

    barrier = pltpu.get_barrier_semaphore()
    each(1, count, lambda peer, device: pl.semaphore_signal(
        barrier, inc=1, device_id=device, device_id_type=MESH))
    query_copy.wait()
    pl.semaphore_wait(barrier, count - 1)
    each(1, members, lambda peer, device: send(gathered.at[me], gathered.at[me], 0, device))

    page_copy.wait()
    positive_copy.wait()
    page_rows = page[...]
    page_columns = page_rows.T
    page_parts = split(page_rows)
    rows[...] = jnp.zeros_like(rows)

    def score(b, logit_row):
        for q in range(block):
            rows[b, q * pad:q * pad + tokens, :] = gathered[b * block + q]
        scores = jnp.dot(
            rows[b], page_columns, precision=highest, preferred_element_type=jnp.float32
        )
        tangent = jnp.tanh(scores / cap_value)
        grid = jnp.exp(tangent * (cap_value / sharpness_divisor))
        totals = jnp.sum(grid, axis=1, keepdims=True)
        peak = sharpness_divisor * jnp.log(totals)
        slopes = grid * (1.0 - tangent * tangent) * ((logit_scale / tokens) / totals)
        term = dot3(split(slopes), page_parts)
        for q in range(block):
            terms[b * block + q] = term[q * pad:q * pad + tokens, :]
        slopes_t[b] = slopes.T
        row = lax.broadcasted_iota(jnp.int32, (block_rows, lanes), 0)
        lane = lax.broadcasted_iota(jnp.int32, (block_rows, lanes), 1)
        mine = (lane == b * block + row // pad) & (row % pad < tokens)
        return logit_row + jnp.sum(jnp.where(mine, peak, 0.0), axis=0, keepdims=True)

    def score_from(s, logit_row):
        return score(lax.rem(group * group_blocks + s, blocks), logit_row)

    def send_term(peer, device):
        send(terms.at[peer], arrived.at[me], 3, device)

    wait_all(gathered, members - 1, recv_sems.at[0])
    own_group = gathered.at[pl.ds(group * members, members)]

    def pass_on(k, carry):
        send(own_group, own_group, 1, (lax.rem(group + k, groups), member))
        return carry

    lax.fori_loop(1, groups, pass_on, 0)
    logit_row = jnp.zeros((1, lanes), jnp.float32)
    logit_row = lax.fori_loop(0, group_blocks, score_from, logit_row)
    each(1, members, send_term)
    wait_all(gathered, count - members, recv_sems.at[1])
    logit_row = lax.fori_loop(group_blocks, blocks, score_from, logit_row)
    own_logits[...] = logit_row * (logit_scale / tokens)
    logits[me] = own_logits[...]
    each(1, count, lambda peer, device: send(own_logits, logits.at[me], 2, device))
    each(members, count, send_term)

    wait_all(logits, count - 1, recv_sems.at[2])
    table = logits[:, 0, :][:, :count]
    of_page = lax.broadcasted_iota(jnp.int32, (count, count), 0)
    of_query = lax.broadcasted_iota(jnp.int32, (count, count), 1)
    chosen = (positive[...] == of_page).astype(jnp.float32)
    grid = jnp.exp(table)
    totals = jnp.sum(grid, axis=0, keepdims=True)
    log_totals = jnp.log(totals)
    matching = jnp.sum(chosen * table, axis=0, keepdims=True)
    losses = log_totals - matching + z_weight * log_totals * log_totals
    loss = jnp.sum(losses, axis=1, keepdims=True) / count
    query_grad[tokens] = jnp.broadcast_to(loss, query_grad.shape[1:])
    coefficients = ((1.0 + 2.0 * z_weight * log_totals) * grid / totals - chosen) / count
    of_me = jnp.sum(jnp.where(of_page == me, coefficients, 0.0), axis=0, keepdims=True)
    to_me = jnp.sum(jnp.where(of_query == me, coefficients, 0.0), axis=1, keepdims=True)
    weights[...] = jnp.broadcast_to(to_me, weights.shape)

    def gather_page(b, total):
        row = lax.broadcasted_iota(jnp.int32, (block_rows, count), 0)
        lane = lax.broadcasted_iota(jnp.int32, (block_rows, count), 1)
        mine = lane == b * block + row // pad
        factor = jnp.sum(jnp.where(mine, of_me, 0.0), axis=1, keepdims=True)
        return total + dot3(split(slopes_t[b]), split(rows[b] * factor))

    page_grad[...] = lax.fori_loop(0, blocks, gather_page, jnp.zeros(page_grad.shape, jnp.float32))

    wait_all(arrived, count - 1, recv_sems.at[3])
    arrived[me] = terms[me]

    def gather_query(p, total):
        return total + arrived[p] * weights[pl.ds(p, 1), :]

    total = lax.fori_loop(
        0, count, gather_query, jnp.zeros(arrived.shape[1:], jnp.float32), unroll=8
    )
    for i in range(tokens):
        query_grad[i] = total[i:i + 1, :]
    wait_all(gathered, members - 1, send_sems.at[0])
    wait_all(gathered, count - members, send_sems.at[1])
    wait_all(logits, count - 1, send_sems.at[2])
    wait_all(terms, count - 1, send_sems.at[3])


def hand_over(query_grad, page_grad, loss_hbm, query_grad_hbm, page_grad_hbm, loss, sems):
    tokens = query_grad_hbm.shape[0]
    page_out = pltpu.make_async_copy(page_grad, page_grad_hbm.at[0], sems.at[0])
    query_out = pltpu.make_async_copy(
        query_grad.at[pl.ds(0, tokens)], query_grad_hbm, sems.at[1]
    )
    loss_out = pltpu.make_async_copy(loss, loss_hbm, sems.at[2])
    page_out.start()
    query_out.start()
    loss[...] = query_grad[tokens][:, :1]
    loss_out.start()
    page_out.wait()
    query_out.wait()
    loss_out.wait()


def shards(groups, members, queries, pages, positive):
    count = groups * members
    _, tokens, width = queries.shape
    page_tokens = pages.shape[1]
    block = math.gcd(members, 16)
    blocks = count // block
    pad = -(-tokens // 8) * 8
    lanes = max(128, -(-count // 128) * 128)
    anywhere = pl.BlockSpec(memory_space=pl.ANY)
    vmem = pl.BlockSpec(memory_space=pltpu.VMEM)
    float32 = jnp.float32
    results = pl.pallas_call(
        functools.partial(kernel, groups, members, block, pad),
        out_shape=(
            pltpu.VMEM((tokens + 1, 1, width), float32),
            pltpu.VMEM((page_tokens, width), float32),
        ),
        in_specs=[anywhere] * 3,
        out_specs=(vmem,) * 2,
        scratch_shapes=[
            pltpu.VMEM((count, tokens, width), float32),
            pltpu.VMEM((page_tokens, width), float32),
            pltpu.VMEM((1, count), jnp.int32),
            pltpu.VMEM((blocks, block * pad, width), float32),
            pltpu.VMEM((blocks, page_tokens, block * pad), float32),
            pltpu.VMEM((1, lanes), float32),
            pltpu.VMEM((count, 1, lanes), float32),
            pltpu.VMEM((count, tokens, width), float32),
            pltpu.VMEM((count, tokens, width), float32),
            pltpu.VMEM((count, width), float32),
            pltpu.SemaphoreType.DMA,
            pltpu.SemaphoreType.DMA,
            pltpu.SemaphoreType.DMA,
            pltpu.SemaphoreType.DMA((4,)),
            pltpu.SemaphoreType.DMA((4,)),
        ],
        compiler_params=pltpu.CompilerParams(collective_id=0, has_side_effects=True),
    )(jnp.transpose(queries, (1, 0, 2)), pages, positive.reshape(1, count))
    loss, query_grad, page_grad = pl.pallas_call(
        hand_over,
        out_shape=(
            jax.ShapeDtypeStruct((1, 1), float32),
            jax.ShapeDtypeStruct((tokens, 1, width), float32),
            jax.ShapeDtypeStruct(pages.shape, float32),
        ),
        in_specs=[vmem] * 2,
        out_specs=(anywhere,) * 3,
        scratch_shapes=[pltpu.VMEM((1, 1), float32), pltpu.SemaphoreType.DMA((3,))],
        compiler_params=pltpu.CompilerParams(vmem_limit_bytes=1 << 20),
    )(*[pltpu.with_memory_space_constraint(x, pltpu.VMEM) for x in results])
    return loss.reshape(()), jnp.transpose(query_grad, (1, 0, 2)), page_grad


def solution(mesh):
    groups, members = mesh.shape["grp"], mesh.shape["dev"]
    split_spec = P(("grp", "dev"), None, None)
    return jax.shard_map(
        functools.partial(shards, groups, members),
        mesh=mesh,
        in_specs=(split_spec, split_spec, P()),
        out_specs=(P(), split_spec, split_spec),
        check_vma=False,
    )
```

time: 29.7 us -> 21.7 us (0.73)
  local copies, waits for them, and re-layouts: 4.16 us -> 0 us
  Pallas kernels: 22.8 us -> 20.9 us
  between operations: 2.4 us -> 0.64 us
    unnamed x3 -> x0, local copies, waits for them, and re-layouts: 4.16 us -> none
    pallas_call x1, Pallas kernels: 22.8 us -> 20.2 us  [shards(): pl.pallas_call(functools.partial(kernel, groups, members, block, pad), ou...]
    pallas_call x0 -> x1, Pallas kernels: none -> 0.69 us  [shards(): pl.pallas_call(hand_over, out_shape=(jax.ShapeDtypeStruct((1, 1), float32...]
where the time goes in v2:
time: 21.7 us; the launch traced here: 21.5 us
  Pallas kernels  20.9 us (96%)
  between operations  0.64 us (3%)
    pallas_call x1, Pallas kernels, shards(): pl.pallas_call(functools.partial(kernel, groups, members, block, pad), ou...  20.2 us
    pallas_call x1, Pallas kernels, shards(): pl.pallas_call(hand_over, out_shape=(jax.ShapeDtypeStruct((1, 1), float32...  0.69 us

profile of v2, /device:TPU:0, one launch (start us, length us, event | category | flops | bytes accessed | tf_op | source)
XLA Modules:
  0.0 21.5 jit_solution(7857365273488504902)
XLA Ops:
  0.6 20.2 %shard_map.58 = (f32[13,1,128]{2,1,0:T(1,128)S(1)}, f32[256,128]{1,0:T(8,128)S(1)}) custom-call(f32[12,1,128]{2,1,0:T(1,128)} %bitcast.4, f32[1,256,128]{2,1,0:T(8,128)} %page_hbm.1, s32[1,32]{1,0:T(1,128)} %bitcast.5), custom_call_target="tpu_custom_call" | custom-call | tf_op jit(solution)/shard_map/pallas_call | solution.py:204
  20.8 0.7 %shard_map.59 = (f32[1,1]{1,0:T(1,128)}, f32[12,1,128]{2,1,0:T(1,128)}, f32[1,256,128]{2,1,0:T(8,128)}) custom-call(f32[13,1,128]{2,1,0:T(1,128)S(1)} %get-tuple-element.8.query_grad, f32[256,128]{1,0:T(8,128)S(1)} %get-tuple-element.9.page_grad), custom_call_target="tpu_custom_call" | custom-call | tf_op jit(solution)/shard_map/pallas_call | solution.py:231

commit v3 on v2

--- a/solution.py
+++ b/solution.py
@@ -35,19 +35,23 @@
     groups, members, block, pad,
     query_hbm, page_hbm, positive_hbm,
     query_grad, page_grad,
-    gathered, page, positive, rows, slopes_t, own_logits, logits, terms, arrived, weights,
+    gathered, page, positive, rows, slopes_of, slopes_t, own_logits, logits, terms, arrived, weights,
     query_sem, page_sem, positive_sem, send_sems, recv_sems,
 ):
     count = groups * members
     group_blocks = members // block
     blocks = groups * group_blocks
-    tokens = gathered.shape[1]
+    _, lines, spots, tokens, _ = gathered.shape
     lanes = own_logits.shape[-1]
     block_rows = block * pad
     group, member = lax.axis_index("grp"), lax.axis_index("dev")
     me = group * members + member
-
-    query_copy = pltpu.make_async_copy(query_hbm.at[:, 0], gathered.at[me], query_sem)
+    line, spot = member // spots, lax.rem(member, spots)
+    own_query = gathered.at[group, line, spot]
+    own_line = gathered.at[group, :, spot]
+    own_group = gathered.at[group]
+
+    query_copy = pltpu.make_async_copy(query_hbm.at[:, 0], own_query, query_sem)
     page_copy = pltpu.make_async_copy(page_hbm.at[0], page, page_sem)
     positive_copy = pltpu.make_async_copy(positive_hbm, positive, positive_sem)
     query_copy.start()
@@ -69,16 +73,43 @@
             device_id=device, device_id_type=MESH,
         ).start()
 
+    def wait_for(whole, sem):
+        pltpu.make_async_copy(whole, whole, sem).wait()
+
     def wait_all(buffer, size, sem):
-        whole = buffer.at[pl.ds(0, size)]
-        pltpu.make_async_copy(whole, whole, sem).wait()
+        wait_for(buffer.at[pl.ds(0, size)], sem)
+
+    def on_line(k):
+        return group, lax.rem(line + k, lines) * spots + spot
+
+    def on_spot(k):
+        return group, line * spots + lax.rem(spot + k, spots)
+
+    def on_group(k):
+        return lax.rem(group + k, groups), member
+
+    def partners(size, of, act):
+        def step(k, carry):
+            act(of(k))
+            return carry
+
+        lax.fori_loop(1, size, step, 0)
+
+    first_part = gathered.at[0, pl.ds(0, lines - 1), 0]
+    second_part = gathered.at[0, :, pl.ds(0, spots - 1)]
+    third_part = gathered.at[pl.ds(0, groups - 1)]
 
     barrier = pltpu.get_barrier_semaphore()
-    each(1, count, lambda peer, device: pl.semaphore_signal(
-        barrier, inc=1, device_id=device, device_id_type=MESH))
+
+    def greet(device):
+        pl.semaphore_signal(barrier, inc=1, device_id=device, device_id_type=MESH)
+
+    partners(lines, on_line, greet)
+    partners(spots, on_spot, greet)
+    partners(groups, on_group, greet)
     query_copy.wait()
-    pl.semaphore_wait(barrier, count - 1)
-    each(1, members, lambda peer, device: send(gathered.at[me], gathered.at[me], 0, device))
+    pl.semaphore_wait(barrier, lines + spots + groups - 3)
+    partners(lines, on_line, lambda device: send(own_query, own_query, 0, device))
 
     page_copy.wait()
     positive_copy.wait()
@@ -87,9 +118,13 @@
     page_parts = split(page_rows)
     rows[...] = jnp.zeros_like(rows)
 
-    def score(b, logit_row):
+    def score(s, logit_row):
+        b = lax.rem(group * group_blocks + s, blocks)
+        first_line = lax.rem(b, group_blocks) * (block // spots)
         for q in range(block):
-            rows[b, q * pad:q * pad + tokens, :] = gathered[b * block + q]
+            rows[b, q * pad:q * pad + tokens, :] = gathered[
+                b // group_blocks, first_line + q // spots, q % spots
+            ]
         scores = jnp.dot(
             rows[b], page_columns, precision=highest, preferred_element_type=jnp.float32
         )
@@ -97,41 +132,41 @@
         grid = jnp.exp(tangent * (cap_value / sharpness_divisor))
         totals = jnp.sum(grid, axis=1, keepdims=True)
         peak = sharpness_divisor * jnp.log(totals)
-        slopes = grid * (1.0 - tangent * tangent) * ((logit_scale / tokens) / totals)
+        slopes_of[b] = grid * (1.0 - tangent * tangent) * ((logit_scale / tokens) / totals)
+        row = lax.broadcasted_iota(jnp.int32, (block_rows, lanes), 0)
+        lane = lax.broadcasted_iota(jnp.int32, (block_rows, lanes), 1)
+        mine = (lane == b * block + row // pad) & (row % pad < tokens)
+        return logit_row + jnp.sum(jnp.where(mine, peak, 0.0), axis=0, keepdims=True)
+
+    def project(s, carry):
+        b = lax.rem(group * group_blocks + s, blocks)
+        slopes = slopes_of[b]
         term = dot3(split(slopes), page_parts)
         for q in range(block):
             terms[b * block + q] = term[q * pad:q * pad + tokens, :]
         slopes_t[b] = slopes.T
-        row = lax.broadcasted_iota(jnp.int32, (block_rows, lanes), 0)
-        lane = lax.broadcasted_iota(jnp.int32, (block_rows, lanes), 1)
-        mine = (lane == b * block + row // pad) & (row % pad < tokens)
-        return logit_row + jnp.sum(jnp.where(mine, peak, 0.0), axis=0, keepdims=True)
-
-    def score_from(s, logit_row):
-        return score(lax.rem(group * group_blocks + s, blocks), logit_row)
+        return carry
 
     def send_term(peer, device):
-        send(terms.at[peer], arrived.at[me], 3, device)
-
-    wait_all(gathered, members - 1, recv_sems.at[0])
-    own_group = gathered.at[pl.ds(group * members, members)]
-
-    def pass_on(k, carry):
-        send(own_group, own_group, 1, (lax.rem(group + k, groups), member))
-        return carry
-
-    lax.fori_loop(1, groups, pass_on, 0)
+        send(terms.at[peer], arrived.at[me], 4, device)
+
+    wait_for(first_part, recv_sems.at[0])
+    partners(spots, on_spot, lambda device: send(own_line, own_line, 1, device))
+    wait_for(second_part, recv_sems.at[1])
+    partners(groups, on_group, lambda device: send(own_group, own_group, 2, device))
     logit_row = jnp.zeros((1, lanes), jnp.float32)
-    logit_row = lax.fori_loop(0, group_blocks, score_from, logit_row)
-    each(1, members, send_term)
-    wait_all(gathered, count - members, recv_sems.at[1])
-    logit_row = lax.fori_loop(group_blocks, blocks, score_from, logit_row)
+    logit_row = lax.fori_loop(0, group_blocks, score, logit_row)
+    lax.fori_loop(0, group_blocks, project, 0)
+    wait_for(third_part, recv_sems.at[2])
+    logit_row = lax.fori_loop(group_blocks, blocks, score, logit_row)
     own_logits[...] = logit_row * (logit_scale / tokens)
     logits[me] = own_logits[...]
-    each(1, count, lambda peer, device: send(own_logits, logits.at[me], 2, device))
+    each(1, count, lambda peer, device: send(own_logits, logits.at[me], 3, device))
+    each(1, members, send_term)
+    lax.fori_loop(group_blocks, blocks, project, 0)
     each(members, count, send_term)
 
-    wait_all(logits, count - 1, recv_sems.at[2])
+    wait_all(logits, count - 1, recv_sems.at[3])
     table = logits[:, 0, :][:, :count]
     of_page = lax.broadcasted_iota(jnp.int32, (count, count), 0)
     of_query = lax.broadcasted_iota(jnp.int32, (count, count), 1)
@@ -157,7 +192,7 @@
 
     page_grad[...] = lax.fori_loop(0, blocks, gather_page, jnp.zeros(page_grad.shape, jnp.float32))
 
-    wait_all(arrived, count - 1, recv_sems.at[3])
+    wait_all(arrived, count - 1, recv_sems.at[4])
     arrived[me] = terms[me]
 
     def gather_query(p, total):
@@ -168,10 +203,11 @@
     )
     for i in range(tokens):
         query_grad[i] = total[i:i + 1, :]
-    wait_all(gathered, members - 1, send_sems.at[0])
-    wait_all(gathered, count - members, send_sems.at[1])
-    wait_all(logits, count - 1, send_sems.at[2])
-    wait_all(terms, count - 1, send_sems.at[3])
+    wait_for(first_part, send_sems.at[0])
+    wait_for(second_part, send_sems.at[1])
+    wait_for(third_part, send_sems.at[2])
+    wait_all(logits, count - 1, send_sems.at[3])
+    wait_all(terms, count - 1, send_sems.at[4])
 
 
 def hand_over(query_grad, page_grad, loss_hbm, query_grad_hbm, page_grad_hbm, loss, sems):
@@ -195,6 +231,7 @@
     _, tokens, width = queries.shape
     page_tokens = pages.shape[1]
     block = math.gcd(members, 16)
+    spots = math.gcd(members, 4)
     blocks = count // block
     pad = -(-tokens // 8) * 8
     lanes = max(128, -(-count // 128) * 128)
@@ -210,10 +247,11 @@
         in_specs=[anywhere] * 3,
         out_specs=(vmem,) * 2,
         scratch_shapes=[
-            pltpu.VMEM((count, tokens, width), float32),
+            pltpu.VMEM((groups, members // spots, spots, tokens, width), float32),
             pltpu.VMEM((page_tokens, width), float32),
             pltpu.VMEM((1, count), jnp.int32),
             pltpu.VMEM((blocks, block * pad, width), float32),
+            pltpu.VMEM((blocks, block * pad, page_tokens), float32),
             pltpu.VMEM((blocks, page_tokens, block * pad), float32),
             pltpu.VMEM((1, lanes), float32),
             pltpu.VMEM((count, 1, lanes), float32),
@@ -223,8 +261,8 @@
             pltpu.SemaphoreType.DMA,
             pltpu.SemaphoreType.DMA,
             pltpu.SemaphoreType.DMA,
-            pltpu.SemaphoreType.DMA((4,)),
-            pltpu.SemaphoreType.DMA((4,)),
+            pltpu.SemaphoreType.DMA((5,)),
+            pltpu.SemaphoreType.DMA((5,)),
         ],
         compiler_params=pltpu.CompilerParams(collective_id=0, has_side_effects=True),
     )(jnp.transpose(queries, (1, 0, 2)), pages, positive.reshape(1, count))

time: 21.7 us -> 22.6 us (1.041)
  the two profiles are of different devices: /device:TPU:0 before, /device:TPU:1 now
where the time goes in v3:
time: 22.6 us; the launch traced here: 22.4 us
  Pallas kernels  21.8 us (96%)
  between operations  0.64 us (3%)
    pallas_call x1, Pallas kernels, shards(): pl.pallas_call(functools.partial(kernel, groups, members, block, pad), ou...  21.1 us
    pallas_call x1, Pallas kernels, shards(): pl.pallas_call(hand_over, out_shape=(jax.ShapeDtypeStruct((1, 1), float32...  0.69 us

profile of v3, /device:TPU:1, one launch (start us, length us, event | category | flops | bytes accessed | tf_op | source)
XLA Modules:
  0.0 22.4 jit_solution(16558356213692481319)
XLA Ops:
  0.6 21.1 %shard_map.58 = (f32[13,1,128]{2,1,0:T(1,128)S(1)}, f32[256,128]{1,0:T(8,128)S(1)}) custom-call(f32[12,1,128]{2,1,0:T(1,128)} %bitcast.4, f32[1,256,128]{2,1,0:T(8,128)} %page_hbm.1, s32[1,32]{1,0:T(1,128)} %bitcast.5), custom_call_target="tpu_custom_call" | custom-call | tf_op jit(solution)/shard_map/pallas_call | solution.py:241
  21.7 0.7 %shard_map.59 = (f32[1,1]{1,0:T(1,128)}, f32[12,1,128]{2,1,0:T(1,128)}, f32[1,256,128]{2,1,0:T(8,128)}) custom-call(f32[13,1,128]{2,1,0:T(1,128)S(1)} %get-tuple-element.8.query_grad, f32[256,128]{1,0:T(8,128)S(1)} %get-tuple-element.9.page_grad), custom_call_target="tpu_custom_call" | custom-call | tf_op jit(solution)/shard_map/pallas_call | solution.py:269

commit v4 on v2

--- a/solution.py
+++ b/solution.py
@@ -35,7 +35,7 @@
     groups, members, block, pad,
     query_hbm, page_hbm, positive_hbm,
     query_grad, page_grad,
-    gathered, page, positive, rows, slopes_t, own_logits, logits, terms, arrived, weights,
+    gathered, page, positive, rows, slopes_of, slopes_t, own_logits, logits, terms, arrived, weights,
     query_sem, page_sem, positive_sem, send_sems, recv_sems,
 ):
     count = groups * members
@@ -74,10 +74,18 @@
         pltpu.make_async_copy(whole, whole, sem).wait()
 
     barrier = pltpu.get_barrier_semaphore()
-    each(1, count, lambda peer, device: pl.semaphore_signal(
+    each(1, members, lambda peer, device: pl.semaphore_signal(
         barrier, inc=1, device_id=device, device_id_type=MESH))
+
+    def greet_group(k, carry):
+        pl.semaphore_signal(
+            barrier, inc=1, device_id=(lax.rem(group + k, groups), member), device_id_type=MESH
+        )
+        return carry
+
+    lax.fori_loop(1, groups, greet_group, 0)
     query_copy.wait()
-    pl.semaphore_wait(barrier, count - 1)
+    pl.semaphore_wait(barrier, members + groups - 2)
     each(1, members, lambda peer, device: send(gathered.at[me], gathered.at[me], 0, device))
 
     page_copy.wait()
@@ -87,7 +95,8 @@
     page_parts = split(page_rows)
     rows[...] = jnp.zeros_like(rows)
 
-    def score(b, logit_row):
+    def score(s, logit_row):
+        b = lax.rem(group * group_blocks + s, blocks)
         for q in range(block):
             rows[b, q * pad:q * pad + tokens, :] = gathered[b * block + q]
         scores = jnp.dot(
@@ -97,18 +106,20 @@
         grid = jnp.exp(tangent * (cap_value / sharpness_divisor))
         totals = jnp.sum(grid, axis=1, keepdims=True)
         peak = sharpness_divisor * jnp.log(totals)
-        slopes = grid * (1.0 - tangent * tangent) * ((logit_scale / tokens) / totals)
+        slopes_of[b] = grid * (1.0 - tangent * tangent) * ((logit_scale / tokens) / totals)
+        row = lax.broadcasted_iota(jnp.int32, (block_rows, lanes), 0)
+        lane = lax.broadcasted_iota(jnp.int32, (block_rows, lanes), 1)
+        mine = (lane == b * block + row // pad) & (row % pad < tokens)
+        return logit_row + jnp.sum(jnp.where(mine, peak, 0.0), axis=0, keepdims=True)
+
+    def project(s, carry):
+        b = lax.rem(group * group_blocks + s, blocks)
+        slopes = slopes_of[b]
         term = dot3(split(slopes), page_parts)
         for q in range(block):
             terms[b * block + q] = term[q * pad:q * pad + tokens, :]
         slopes_t[b] = slopes.T
-        row = lax.broadcasted_iota(jnp.int32, (block_rows, lanes), 0)
-        lane = lax.broadcasted_iota(jnp.int32, (block_rows, lanes), 1)
-        mine = (lane == b * block + row // pad) & (row % pad < tokens)
-        return logit_row + jnp.sum(jnp.where(mine, peak, 0.0), axis=0, keepdims=True)
-
-    def score_from(s, logit_row):
-        return score(lax.rem(group * group_blocks + s, blocks), logit_row)
+        return carry
 
     def send_term(peer, device):
         send(terms.at[peer], arrived.at[me], 3, device)
@@ -122,13 +133,15 @@
 
     lax.fori_loop(1, groups, pass_on, 0)
     logit_row = jnp.zeros((1, lanes), jnp.float32)
-    logit_row = lax.fori_loop(0, group_blocks, score_from, logit_row)
+    logit_row = lax.fori_loop(0, group_blocks, score, logit_row)
+    lax.fori_loop(0, group_blocks, project, 0)
     each(1, members, send_term)
     wait_all(gathered, count - members, recv_sems.at[1])
-    logit_row = lax.fori_loop(group_blocks, blocks, score_from, logit_row)
+    logit_row = lax.fori_loop(group_blocks, blocks, score, logit_row)
     own_logits[...] = logit_row * (logit_scale / tokens)
     logits[me] = own_logits[...]
     each(1, count, lambda peer, device: send(own_logits, logits.at[me], 2, device))
+    lax.fori_loop(group_blocks, blocks, project, 0)
     each(members, count, send_term)
 
     wait_all(logits, count - 1, recv_sems.at[2])
@@ -214,6 +227,7 @@
             pltpu.VMEM((page_tokens, width), float32),
             pltpu.VMEM((1, count), jnp.int32),
             pltpu.VMEM((blocks, block * pad, width), float32),
+            pltpu.VMEM((blocks, block * pad, page_tokens), float32),
             pltpu.VMEM((blocks, page_tokens, block * pad), float32),
             pltpu.VMEM((1, lanes), float32),
             pltpu.VMEM((count, 1, lanes), float32),

time: 21.7 us -> 20.8 us (0.959)
  Pallas kernels: 20.9 us -> 20.1 us
    pallas_call x1, Pallas kernels: 20.2 us -> 19.4 us  [shards(): pl.pallas_call(functools.partial(kernel, groups, members, block, pad), ou...]
where the time goes in v4:
time: 20.8 us; the launch traced here: 20.7 us
  Pallas kernels  20.1 us (97%)
  between operations  0.64 us (3%)
    pallas_call x1, Pallas kernels, shards(): pl.pallas_call(functools.partial(kernel, groups, members, block, pad), ou...  19.4 us
    pallas_call x1, Pallas kernels, shards(): pl.pallas_call(hand_over, out_shape=(jax.ShapeDtypeStruct((1, 1), float32...  0.69 us

profile of v4, /device:TPU:0, one launch (start us, length us, event | category | flops | bytes accessed | tf_op | source)
XLA Modules:
  0.0 20.7 jit_solution(14137552147750037951)
XLA Ops:
  0.6 19.4 %shard_map.58 = (f32[13,1,128]{2,1,0:T(1,128)S(1)}, f32[256,128]{1,0:T(8,128)S(1)}) custom-call(f32[12,1,128]{2,1,0:T(1,128)} %bitcast.4, f32[1,256,128]{2,1,0:T(8,128)} %page_hbm.1, s32[1,32]{1,0:T(1,128)} %bitcast.5), custom_call_target="tpu_custom_call" | custom-call | tf_op jit(solution)/shard_map/pallas_call | solution.py:217
  20.0 0.7 %shard_map.59 = (f32[1,1]{1,0:T(1,128)}, f32[12,1,128]{2,1,0:T(1,128)}, f32[1,256,128]{2,1,0:T(8,128)}) custom-call(f32[13,1,128]{2,1,0:T(1,128)S(1)} %get-tuple-element.8.query_grad, f32[256,128]{1,0:T(8,128)S(1)} %get-tuple-element.9.page_grad), custom_call_target="tpu_custom_call" | custom-call | tf_op jit(solution)/shard_map/pallas_call | solution.py:245
